TPU v7x, 128 devices: a whole 4x4x4 slice. The times are simulated.
128 devices in a mesh: paths: 16 (over z, y_lo, core), stocks: 8 (over x, y_hi).
Axes of the slice: x: 4, y: 4 (y_hi: 2, y_lo: 2; y = y_hi * 2 + y_lo), z: 4, core: 2. Of those that a mesh axis runs over, the one named last changes fastest.
Arguments:
- prices: bfloat16 [256, 262144], P('stocks', 'paths'), may hold values from -18 to 18
- loadings: bfloat16 [256, 32], P('stocks'), may hold values from -0.25 to 0.25
- basis_w: float32 [32, 512], replicated, may hold values from -1 to 1
- basis_bias: float32 [512], replicated, may hold values from -1 to 1
- payoff: bfloat16 [262144], P('paths'), may hold values from -4 to 4
- in_fit: int32 [262144], P('paths'), may hold values 0 or 1
- cotangent: bfloat16 [256, 262144], P('stocks', 'paths'), may hold values from -6 to 6
- shocks: bfloat16 [4, 256, 262144], P(None, 'stocks', 'paths'), may hold values from -6 to 6
- corr_gen: bfloat16 [256, 256], replicated, may hold values from -0.375 to 0.375
- basket: float32 [256], replicated, may hold values from 0.2 to 2
- exercise: int32 [4, 262144], P(None, 'paths'), may hold values 0 or 1
- bucket: int32 [4, 262144], P(None, 'paths'), may hold values from 0 to 255
Outputs:
- delta_out: float32 [256, 262144], P('stocks', 'paths')
- surface: float32 [256, 256], P('stocks', 'paths')
All inputs are finite; a program needn't handle non-finite values. No bound on the sum of `in_fit` or of `exercise` on one device may be relied on, other than what follows from the above.
Results may differ from a plain program's by a relative error of at most 0.003.
Values may be sent and summed in bfloat16 or wider, within the bound.
No kernel may reach another device: no remote copies, remote signals or barrier semaphores. Data moves between devices by JAX's collectives and lax.ppermute only.
A program may use at most 192 MiB of HBM per device.

v0:
```python
import jax
import jax.numpy as jnp
from jax import lax
from jax.sharding import PartitionSpec as P

NK = 256
STEPS = 4
time_step = 0.25
ridge_weight = 0.1


def split_up(x, dim, size):
    lengths = x.shape
    pieces = x.reshape(*lengths[:dim], size, lengths[dim] // size, *lengths[dim + 1 :])
    return jnp.moveaxis(pieces, dim, 0)


def sum_at_owner(x, axis, dim):
    size = lax.axis_size(axis)
    pieces = lax.all_to_all(split_up(x, dim, size), axis, 0, 0, tiled=True)
    return jnp.sum(pieces, axis=0)


def piece_ends(length, count):
    unit = 8 if length >= 8 * count else 1
    return [length // unit * k // count * unit for k in range(1, count)]


def joined_along(pieces, dim):
    pieces = jnp.moveaxis(pieces, 0, dim)
    lengths = pieces.shape
    return pieces.reshape(*lengths[:dim], lengths[dim] * lengths[dim + 1], *lengths[dim + 2 :])


def several_exchanges(x, axis, pieces, split_dim, concat_dim):
    blocks = split_up(x, split_dim, lax.axis_size(axis))
    cut = max(range(1, max(2, blocks.ndim - 1)), key=lambda d: blocks.shape[d])
    gathered = []
    for share in jnp.split(blocks, piece_ends(blocks.shape[cut], pieces), axis=cut):
        if share.size:
            gathered.append(lax.all_to_all(share, axis, split_axis=0, concat_axis=0, tiled=True))
    return joined_along(jnp.concatenate(gathered, axis=cut), concat_dim)


def make_basis(factors, basis_w, basis_bias):
    raised = (
        jnp.dot(
            basis_w.T, factors, preferred_element_type=jnp.float32, precision=lax.Precision.HIGHEST
        )
        + basis_bias[:, None]
    )
    return jnp.tanh(raised).astype(jnp.bfloat16)


def regression_sums(basis, payoff, in_fit):
    picked = basis * in_fit.astype(jnp.bfloat16)[None, :]
    gram_sums = lax.dot_general(
        picked, basis, (((1,), (1,)), ((), ())), preferred_element_type=jnp.float32
    )
    moment = jnp.dot(picked, payoff, preferred_element_type=jnp.float32)
    return (gram_sums, moment)


def solve_coefficients(gram_sums, moment, path_count):
    system = gram_sums / path_count + ridge_weight * jnp.eye(gram_sums.shape[0], dtype=jnp.float32)
    cholesky_factor = jnp.linalg.cholesky(system)
    return jax.scipy.linalg.cho_solve((cholesky_factor, True), moment / path_count)


def per_device(
    prices,
    loadings,
    basis_w,
    basis_bias,
    payoff,
    in_fit,
    cotangent,
    shocks,
    corr_gen,
    basket,
    exercise,
    bucket,
):
    stock_count = lax.axis_size("stocks")
    local_paths = prices.shape[1]
    slab_part = local_paths // stock_count
    path_count = float(local_paths * lax.axis_size("paths"))
    offset = lax.axis_index("stocks") * slab_part
    partial_value = lax.dot_general(
        loadings, prices, (((0,), (0,)), ((), ())), preferred_element_type=jnp.float32
    )
    factors_own = sum_at_owner(partial_value, "stocks", 1)
    basis = make_basis(factors_own, basis_w, basis_bias)
    payoff_own = lax.dynamic_slice_in_dim(payoff, offset, slab_part, 0)
    fit_own = lax.dynamic_slice_in_dim(in_fit, offset, slab_part, 0)
    gram_sums, moment = regression_sums(basis, payoff_own, fit_own)
    gram_sums, moment = lax.psum((gram_sums, moment), ("paths", "stocks"))
    coefficients = solve_coefficients(gram_sums, moment, path_count)
    continuation_own = jnp.dot(
        coefficients, basis, preferred_element_type=jnp.float32, precision=lax.Precision.HIGHEST
    )
    strikes = jnp.arange(NK, dtype=jnp.int32)
    stacked = jnp.concatenate([cotangent[None], shocks], axis=0)
    exchanged = several_exchanges(stacked, "stocks", 2, 2, 1)
    exercise_own = lax.dynamic_slice_in_dim(exercise, offset, slab_part, 1)
    bucket_own = lax.dynamic_slice_in_dim(bucket, offset, slab_part, 1)
    adjoint = exchanged[0].astype(jnp.float32)
    partial_surface = jnp.zeros((corr_gen.shape[0], NK), jnp.float32)
    for date_index in range(STEPS - 1, -1, -1):
        mixed_rows = jnp.dot(
            corr_gen, adjoint.astype(jnp.bfloat16), preferred_element_type=jnp.float32
        )
        adjoint = (
            adjoint
            + time_step * mixed_rows
            + exercise_own[date_index].astype(jnp.float32)[None, :]
            * continuation_own[None, :]
            * basket[:, None]
        )
        vega_terms = (adjoint * exchanged[date_index + 1].astype(jnp.float32)).astype(jnp.bfloat16)
        one_hot = (bucket_own[date_index][:, None] == strikes[None, :]).astype(jnp.bfloat16)
        partial_surface = partial_surface + jnp.dot(
            vega_terms, one_hot, preferred_element_type=jnp.float32
        )
    strike_share = sum_at_owner(partial_surface, "paths", 1)
    surface = sum_at_owner(strike_share, "stocks", 0)
    delta_out = lax.all_to_all(adjoint, "stocks", split_axis=0, concat_axis=1, tiled=True)
    return (delta_out, surface)


def solution(mesh):
    return jax.shard_map(
        per_device,
        mesh=mesh,
        in_specs=(
            P("stocks", "paths"),
            P("stocks", None),
            P(),
            P(),
            P("paths"),
            P("paths"),
            P("stocks", "paths"),
            P(None, "stocks", "paths"),
            P(),
            P(),
            P(None, "paths"),
            P(None, "paths"),
        ),
        out_specs=(P("stocks", "paths"), P("stocks", "paths")),
        check_vma=False,
    )
```

profile of v0, /device:TPU:0, one launch (start us, length us, event | category | flops | bytes accessed | tf_op | source)
XLA Modules:
  0.0 493.1 jit_solution(14408656979231489318)
XLA Ops:
  7.2 1.2 copy-done
  8.4 1.2 fusion.108
  9.6 1.5 copy.65
  11.0 7.0 %all-to-all-start.2 = ((f32[8,32,2048]{2,1,0:T(8,128)}), f32[8,32,2048]{2,1,0:T(8,128)}, u32[]{:S(2)}, u32[]{:S(2)}) async-start(f32[8,32,2048]{2,1,0:T(8,128)} %bitcast.220), calls=%async_computation.2 | async-start | bytes 4194304 | tf_op jit(solution)/shard_map/all_to_all | solution.py:20
  18.0 5.1 %copy.62 = bf16[16,8,8,2048]{3,2,1,0:T(8,128)(2,1)S(1)} copy(bf16[16,8,8,2048]{3,1,2,0:T(8,128)(2,1)} %bitcast.237) | data formatting | bytes 8388608
  24.2 2.0 fusion.106
  26.1 2.9 copy.40
  29.1 20.2 %all-to-all-done.2 = f32[8,32,2048]{2,1,0:T(8,128)} async-done(((f32[8,32,2048]{2,1,0:T(8,128)}), f32[8,32,2048]{2,1,0:T(8,128)}, u32[]{:S(2)}, u32[]{:S(2)}) %all-to-all-start.2) | async-done | bytes 2097184 | tf_op jit(solution)/shard_map/all_to_all | solution.py:20
  49.3 3.6 all-to-all-start
  52.9 4.7 copy.41
  57.6 32.7 %all-to-all-done = bf16[8,5,16,2048]{3,2,1,0:T(8,128)(2,1)S(1)} async-done(((bf16[8,5,16,2048]{3,2,1,0:T(8,128)(2,1)}), bf16[8,5,16,2048]{3,2,1,0:T(8,128)(2,1)S(1)}, u32[]{:S(2)}, u32[]{:S(2)}) %all-to-all-start) | async-done | bytes 2621472 | tf_op jit(solution)/shard_map/all_to_all | solution.py:41
  90.3 4.4 all-to-all-start.1
  95.0 0.7 dynamic_slice.14
  95.7 0.7 dynamic-slice_convert_fusion.4
  96.4 1.7 dynamic-slice_convert_fusion
  98.1 1.7 reduce_sum.27
  99.9 3.8 tanh_convert_fusion
  103.7 1.3 copy-done.9
  105.0 2.5 fusion.19
  107.5 2.0 fusion.18
  109.6 77.3 %psum.15 = f32[512]{0:T(512)S(1)} all-reduce(f32[512]{0:T(512)S(1)} %bitcast.256), channel_id=1, replica_groups=mesh['paths'=16,'stocks'=8] {'paths','stocks'}, use_global_device_ids=true, to_apply=%region_10.11 | all-reduce | flops 512 | bytes 4096 | tf_op jit(solution)/shard_map/psum | solution.py:97
  186.9 2.2 maximum_bitcast_fusion.1
  189.1 2.1 fusion.105
  191.2 73.9 %all-reduce.3.cloned.1.call-done = f32[512,512]{0,1:T(8,128)} async-done(((f32[512,512]{0,1:T(8,128)}), f32[512,512]{0,1:T(8,128)}) %all-reduce.3.cloned.1.call-update) | async-done | bytes 1048592 | tf_op jit(solution)/shard_map/psum | solution.py:97
  265.1 2.4 select_add_fusion
  267.5 1.6 copy.44
  269.3 1.0 copy-done.7
  270.3 11.7 %cholesky.103 = f32[128,128]{1,0:T(8,128)S(1)} custom-call(f32[128,128]{1,0:T(8,128)S(1)} %cholesky.263), custom_call_target="Cholesky" | custom-call | tf_op jit(solution)/shard_map/jit(cholesky)/cholesky | solution.py:66
  282.0 9.8 %custom-call.34 = f32[1,128,128]{1,2,0:T(8,128)S(1)} custom-call(f32[1,128,128]{2,1,0:T(8,128)S(1)} %get-tuple-element.52), custom_call_target="InvertDiagBlocksLowerTriangular" | custom-call | tf_op jit(solution)/shard_map/jit(cholesky)/cholesky | solution.py:66
  291.8 1.2 fusion.57
  293.1 1.3 convolution_subtract_fusion
  294.4 11.7 %cholesky.215 = f32[128,128]{1,0:T(8,128)S(1)} custom-call(f32[128,128]{1,0:T(8,128)S(1)} %cholesky.267), custom_call_target="Cholesky" | custom-call | tf_op jit(solution)/shard_map/jit(cholesky)/cholesky | solution.py:66
  307.0 9.8 %custom-call.35 = f32[1,128,128]{1,2,0:T(8,128)S(1)} custom-call(f32[1,128,128]{2,1,0:T(8,128)S(1)} %get-tuple-element.50), custom_call_target="InvertDiagBlocksLowerTriangular" | custom-call | tf_op jit(solution)/shard_map/jit(cholesky)/cholesky | solution.py:66
  317.1 1.5 convolution_subtract_fusion.1
  318.7 11.7 %cholesky.236 = f32[128,128]{1,0:T(8,128)S(1)} custom-call(f32[128,128]{1,0:T(8,128)S(1)} %cholesky.272), custom_call_target="Cholesky" | custom-call | tf_op jit(solution)/shard_map/jit(cholesky)/cholesky | solution.py:66
  330.5 9.8 %custom-call.36 = f32[1,128,128]{1,2,0:T(8,128)S(1)} custom-call(f32[1,128,128]{2,1,0:T(8,128)S(1)} %get-tuple-element.48), custom_call_target="InvertDiagBlocksLowerTriangular" | custom-call | tf_op jit(solution)/shard_map/jit(cholesky)/cholesky | solution.py:66
  340.6 1.3 convolution_subtract_fusion.2
  342.0 11.9 %cholesky.253 = f32[128,128]{1,0:T(8,128)S(1)} custom-call(f32[128,128]{1,0:T(8,128)S(1)} %convolution_subtract_fusion.2), custom_call_target="Cholesky" | custom-call | tf_op jit(solution)/shard_map/jit(cholesky)/cholesky | solution.py:66
  354.0 0.7 compare_reduce_fusion.1
  354.6 0.7 compare_reduce_fusion
  355.4 0.6 compare_reduce_fusion.2
  358.6 11.2 %while.1 = (s32[]{:T(128)}, f32[512,512]{0,1:T(8,128)S(1)}, s32[4,2]{0,1:T(2,128)S(1)}, f32[4,128,128]{2,1,0:T(8,128)}, s32[]{:T(128)}) while((s32[]{:T(128)}, f32[512,512]{0,1:T(8,128)S(1)}, s32[4,2]{0,1:T(2,128)S(1)}, f32[4,128,128]{2,1,0:T(8,128)}, s32[]{:T(128)}) %tuple.48), condition=%wide.while_cond, body=%wide.while_body.sunk | while | flops 2 | bytes 393829 | solution.py:67
  359.2 1.4 dynamic-slice.23
  360.7 0.6 bitcast_dynamic-update-slice_fusion.2
  362.0 1.4 dynamic-slice.23
  363.5 0.6 bitcast_dynamic-update-slice_fusion.2
  364.8 1.4 dynamic-slice.23
  366.3 0.6 bitcast_dynamic-update-slice_fusion.2
  367.6 1.4 dynamic-slice.23
  369.1 0.6 bitcast_dynamic-update-slice_fusion.2
  369.8 40.2 %custom-call.37 = f32[4,128,128]{1,2,0:T(8,128)S(1)} custom-call(f32[4,128,128]{2,1,0:T(8,128)} %get-tuple-element.9), custom_call_target="InvertDiagBlocksLowerTriangular" | custom-call | tf_op jit(solution)/shard_map/jit(_cho_solve)/triangular_solve | solution.py:67
  412.9 3.4 fusion.16
  417.5 0.7 copy-done.4
  418.2 1.1 fusion.20
  419.8 1.8 fusion.2
  421.6 1.1 fusion.26
  422.8 1.1 fusion.25
  423.9 2.6 fusion.24
  426.5 12.6 %all_to_all.44 = f32[16,256,16]{1,2,0:T(8,128)S(1)} all-to-all(f32[16,256,16]{1,2,0:T(8,128)S(1)} %bitcast.239), channel_id=1, replica_groups=mesh['paths'=16,'stocks'=8] {'paths'}, dimensions={0} | all-to-all | bytes 524288 | tf_op jit(solution)/shard_map/all_to_all | solution.py:20
  439.4 12.8 %all_to_all.45 = f32[8,1,512]{2,1,0:T(1,128)S(1)} all-to-all(f32[8,1,512]{2,1,0:T(1,128)S(1)} %reshape.229), channel_id=1, replica_groups=mesh['paths'=16,'stocks'=8] {'stocks'}, dimensions={0} | all-to-all | bytes 32768 | tf_op jit(solution)/shard_map/all_to_all | solution.py:20
  452.2 3.6 all-to-all-start.3
  456.3 0.7 reduce.24
  457.7 26.7 %all-to-all-done.3 = f32[8,32,2048]{2,1,0:T(8,128)S(1)} async-done(((f32[8,32,2048]{2,1,0:T(8,128)}), f32[8,32,2048]{2,1,0:T(8,128)S(1)}, u32[]{:S(2)}, u32[]{:S(2)}) %all-to-all-start.3) | async-done | bytes 2097184 | tf_op jit(solution)/shard_map/all_to_all | solution.py:127
  484.4 1.5 copy.60
  (106 shorter events, 12.8 us)
Async XLA Ops:
  7.2 1.2 copy-start
  11.0 38.3 %all-to-all-start.2 = ((f32[8,32,2048]{2,1,0:T(8,128)}), f32[8,32,2048]{2,1,0:T(8,128)}, u32[]{:S(2)}, u32[]{:S(2)}) async-start(f32[8,32,2048]{2,1,0:T(8,128)} %bitcast.220), calls=%async_computation.2 | async-start | bytes 4194304 | tf_op jit(solution)/shard_map/all_to_all | solution.py:20
  18.0 5.1 %copy-start.10 = (bf16[32,16384]{1,0:T(8,128)(2,1)S(1)}, bf16[32,16384]{1,0:T(8,128)(2,1)}, u32[]{:S(2)}) copy-start(bf16[32,16384]{1,0:T(8,128)(2,1)} %param.18) | copy-start | bytes 3145732
  49.3 41.0 %all-to-all-start = ((bf16[8,5,16,2048]{3,2,1,0:T(8,128)(2,1)}), bf16[8,5,16,2048]{3,2,1,0:T(8,128)(2,1)S(1)}, u32[]{:S(2)}, u32[]{:S(2)}) async-start(bf16[8,5,16,2048]{3,2,1,0:T(8,128)(2,1)} %copy.40), calls=%async_computation | async-start | bytes 5242880 | tf_op jit(solution)/shard_map/all_to_all | solution.py:41
  90.3 96.6 %all-to-all-start.1 = ((bf16[8,5,16,2048]{3,2,1,0:T(8,128)(2,1)}), bf16[8,5,16,2048]{3,2,1,0:T(8,128)(2,1)}, u32[]{:S(2)}, u32[]{:S(2)}) async-start(bf16[8,5,16,2048]{3,2,1,0:T(8,128)(2,1)} %copy.41), calls=%async_computation.1 | async-start | bytes 5242880 | tf_op jit(solution)/shard_map/all_to_all | solution.py:41
  94.7 5.1 %copy-start.19 = (f32[32,512]{1,0:T(8,128)S(1)}, f32[32,512]{1,0:T(8,128)}, u32[]{:S(2)}) copy-start(f32[32,512]{1,0:T(8,128)} %param.14) | copy-start | bytes 196612
  94.7 5.1 %copy-start.20 = (f32[512]{0:T(512)S(1)}, f32[512]{0:T(512)}, u32[]{:S(2)}) copy-start(f32[512]{0:T(512)} %param.15) | copy-start | bytes 6148
  94.7 170.3 %all-reduce.3.cloned.1.call-start = ((), (), s32[]{:S(2)}) async-start(), calls=%async_computation.6 | async-start | bytes 2097152 | tf_op jit(solution)/shard_map/psum | solution.py:97
  103.7 1.3 copy-start.9
  265.1 4.0 copy-start.6
  269.3 1.0 copy-start.7
  369.7 46.6 %copy-start.5 = (bf16[1,8,32,2048]{3,2,0,1:T(8,128)(2,1)S(1)}, bf16[1,8,32,2048]{3,2,0,1:T(8,128)(2,1)}, u32[]{:S(2)}) copy-start(bf16[1,8,32,2048]{3,2,0,1:T(8,128)(2,1)} %get-tuple-element.36) | copy-start | bytes 3145732
  369.7 46.6 %copy-start.8 = (bf16[256,256]{1,0:T(8,128)(2,1)S(1)}, bf16[256,256]{1,0:T(8,128)(2,1)}, u32[]{:S(2)}) copy-start(bf16[256,256]{1,0:T(8,128)(2,1)} %param.20) | copy-start | bytes 393220
  369.8 46.6 %copy-start.18 = (f32[256]{0:T(256)S(1)}, f32[256]{0:T(256)}, u32[]{:S(2)}) copy-start(f32[256]{0:T(256)} %param.21) | copy-start | bytes 3076
  410.0 6.3 %copy-start.14 = (f32[1,2048]{1,0:T(1,128)S(1)}, f32[1,2048]{1,0:T(1,128)}, u32[]{:S(2)}) copy-start(f32[1,2048]{1,0:T(1,128)} %get-tuple-element.43) | copy-start | bytes 24580
  410.0 6.3 %copy-start.15 = (f32[1,2048]{1,0:T(1,128)S(1)}, f32[1,2048]{1,0:T(1,128)}, u32[]{:S(2)}) copy-start(f32[1,2048]{1,0:T(1,128)} %get-tuple-element.44) | copy-start | bytes 24580
  410.0 6.3 %copy-start.16 = (f32[1,2048]{1,0:T(1,128)S(1)}, f32[1,2048]{1,0:T(1,128)}, u32[]{:S(2)}) copy-start(f32[1,2048]{1,0:T(1,128)} %get-tuple-element.45) | copy-start | bytes 24580
  410.0 6.3 %copy-start.17 = (f32[1,2048]{1,0:T(1,128)S(1)}, f32[1,2048]{1,0:T(1,128)}, u32[]{:S(2)}) copy-start(f32[1,2048]{1,0:T(1,128)} %get-tuple-element.46) | copy-start | bytes 24580
  416.9 1.2 copy-start.4
  416.9 1.2 copy-start.13
  419.7 1.9 copy-start.3
  419.8 1.8 copy-start.12
  421.6 1.2 copy-start.2
  421.6 1.2 copy-start.11
  452.2 32.2 %all-to-all-start.3 = ((f32[8,32,2048]{2,1,0:T(8,128)}), f32[8,32,2048]{2,1,0:T(8,128)S(1)}, u32[]{:S(2)}, u32[]{:S(2)}) async-start(f32[8,32,2048]{2,1,0:T(8,128)} %bitcast.60), calls=%async_computation.3 | async-start | bytes 4194304 | tf_op jit(solution)/shard_map/all_to_all | solution.py:127
  484.4 1.6 copy-start.1
Sparse Core Ops, SparseCore 0:
  107.6 157.3 all-reduce.2
where the time goes:
time: 501 us; the launch traced here: 493 us
  waiting for transfers between devices  154 us (31%)
  other arithmetic  130 us (26%)
  blocking collectives  103 us (21%)
  local copies, waits for them, and re-layouts  40 us (8%)
  matrix products  30.9 us (6%)
  starting transfers between devices  18.9 us (4%)
  between operations  17.2 us (3%)
    another operation x14, other arithmetic, solve_coefficients(): cholesky_factor = jnp.linalg.cholesky(system)  78.6 us
    psum x1, blocking collectives, per_device(): gram_sums, moment = lax.psum((gram_sums, moment), ('paths', 'stocks'))  77.3 us
    psum x1, waiting for transfers between devices, per_device(): gram_sums, moment = lax.psum((gram_sums, moment), ('paths', 'stocks'))  73.9 us
    another operation x3, other arithmetic, solve_coefficients(): jax.scipy.linalg.cho_solve((cholesky_factor, True), moment / path_count)  40.3 us
    all_to_all x2, waiting for transfers between devices, several_exchanges(): lax.all_to_all(share, axis, split_axis=0, concat_axis=0, tiled=True)  32.7 us
    all_to_all x1, waiting for transfers between devices, per_device(): lax.all_to_all(adjoint, 'stocks', split_axis=0, concat_axis=1, tiled=True)  26.7 us
    all_to_all x2, blocking collectives, sum_at_owner(): pieces = lax.all_to_all(split_up(x, dim, size), axis, 0, 0, tiled=True)  25.4 us
    all_to_all x1, waiting for transfers between devices, sum_at_owner(): pieces = lax.all_to_all(split_up(x, dim, size), axis, 0, 0, tiled=True)  20.2 us
  transfers between devices with their start and end apart: 5, of which 4 were waited for; matrix products, arithmetic and copies ran while one was open for 7% of the time, Pallas kernels for 0%

commit v1 on v0

--- a/solution.py
+++ b/solution.py
@@ -94,7 +94,7 @@
     payoff_own = lax.dynamic_slice_in_dim(payoff, offset, slab_part, 0)
     fit_own = lax.dynamic_slice_in_dim(in_fit, offset, slab_part, 0)
     gram_sums, moment = regression_sums(basis, payoff_own, fit_own)
-    gram_sums, moment = lax.psum((gram_sums, moment), ("paths", "stocks"))
+    gram_sums, moment = lax.psum(lax.psum((gram_sums, moment), "stocks"), "paths")
     coefficients = solve_coefficients(gram_sums, moment, path_count)
     continuation_own = jnp.dot(
         coefficients, basis, preferred_element_type=jnp.float32, precision=lax.Precision.HIGHEST

time: 501 us -> 565 us (1.13)
  waiting for transfers between devices: 154 us -> 226 us
  blocking collectives: 103 us -> 92.9 us
    psum x1 -> x2, waiting for transfers between devices: 73.9 us -> 147 us  [the longest x1 116 us: per_device(): lax.psum(lax.psum((gram_sums, moment), 'stocks'), 'paths')]
    psum x1 -> x2, blocking collectives: 77.3 us -> 66.4 us  [the longest x1 35.4 us: per_device(): lax.psum((gram_sums, moment), 'stocks')]
  transfers between devices with their start and end apart: 5 -> 6, of which waited for: 4 -> 5; matrix products, arithmetic and copies ran while one was open for 7% -> 6% of each run, Pallas kernels for 0% -> 0%
where the time goes in v1:
time: 565 us; the launch traced here: 555 us
  waiting for transfers between devices  226 us (40%)
  other arithmetic  130 us (23%)
  blocking collectives  92.9 us (16%)
  local copies, waits for them, and re-layouts  38.6 us (7%)
  matrix products  31 us (5%)
  starting transfers between devices  18.7 us (3%)
  between operations  17.5 us (3%)
    psum x1, waiting for transfers between devices, per_device(): lax.psum(lax.psum((gram_sums, moment), 'stocks'), 'paths')  116 us
    another operation x14, other arithmetic, solve_coefficients(): cholesky_factor = jnp.linalg.cholesky(system)  78.6 us
    another operation x3, other arithmetic, solve_coefficients(): jax.scipy.linalg.cho_solve((cholesky_factor, True), moment / path_count)  40.3 us
    psum x1, blocking collectives, per_device(): lax.psum((gram_sums, moment), 'stocks')  35.4 us
    all_to_all x2, waiting for transfers between devices, several_exchanges(): lax.all_to_all(share, axis, split_axis=0, concat_axis=0, tiled=True)  32.7 us
    psum x1, blocking collectives, per_device(): lax.psum(lax.psum((gram_sums, moment), 'stocks'), 'paths')  30.9 us
    psum x1, waiting for transfers between devices, per_device(): lax.psum((gram_sums, moment), 'stocks')  30.4 us
    all_to_all x1, waiting for transfers between devices, per_device(): lax.all_to_all(adjoint, 'stocks', split_axis=0, concat_axis=1, tiled=True)  26.7 us
  transfers between devices with their start and end apart: 6, of which 5 were waited for; matrix products, arithmetic and copies ran while one was open for 6% of the time, Pallas kernels for 0%

profile of v1, /device:TPU:0, one launch (start us, length us, event | category | flops | bytes accessed | tf_op | source)
XLA Modules:
  0.0 554.8 jit_solution(9560813853234308752)
XLA Ops:
  7.2 1.2 copy-done
  8.4 1.2 fusion.108
  9.6 1.5 copy.65
  11.1 7.0 %all-to-all-start.2 = ((f32[8,32,2048]{2,1,0:T(8,128)}), f32[8,32,2048]{2,1,0:T(8,128)}, u32[]{:S(2)}, u32[]{:S(2)}) async-start(f32[8,32,2048]{2,1,0:T(8,128)} %bitcast.220), calls=%async_computation.2 | async-start | bytes 4194304 | tf_op jit(solution)/shard_map/all_to_all | solution.py:20
  18.0 5.1 copy.62
  24.2 2.0 fusion.106
  26.2 2.9 copy.40
  29.1 20.2 %all-to-all-done.2 = f32[8,32,2048]{2,1,0:T(8,128)} async-done(((f32[8,32,2048]{2,1,0:T(8,128)}), f32[8,32,2048]{2,1,0:T(8,128)}, u32[]{:S(2)}, u32[]{:S(2)}) %all-to-all-start.2) | async-done | bytes 2097184 | tf_op jit(solution)/shard_map/all_to_all | solution.py:20
  49.3 3.6 all-to-all-start
  53.0 4.7 copy.41
  57.6 32.7 %all-to-all-done = bf16[8,5,16,2048]{3,2,1,0:T(8,128)(2,1)S(1)} async-done(((bf16[8,5,16,2048]{3,2,1,0:T(8,128)(2,1)}), bf16[8,5,16,2048]{3,2,1,0:T(8,128)(2,1)S(1)}, u32[]{:S(2)}, u32[]{:S(2)}) %all-to-all-start) | async-done | bytes 2621472 | tf_op jit(solution)/shard_map/all_to_all | solution.py:41
  90.4 4.4 all-to-all-start.1
  94.8 0.7 dynamic-slice_convert_fusion.4
  95.5 1.7 reduce_sum.27
  97.3 3.9 tanh_convert_fusion
  101.2 1.3 copy-done.9
  102.5 2.5 fusion.19
  105.1 1.7 dynamic-slice_convert_fusion
  106.8 2.0 fusion.18
  108.8 35.4 %psum.30 = f32[512]{0:T(512)S(1)} all-reduce(f32[512]{0:T(512)S(1)} %bitcast.256), channel_id=1, replica_groups=mesh['paths'=16,'stocks'=8] {'stocks'}, use_global_device_ids=true, to_apply=%region_11.12 | all-reduce | flops 512 | bytes 4096 | tf_op jit(solution)/shard_map/psum | solution.py:97
  144.3 30.9 %psum.31 = f32[512]{0:T(512)S(1)} all-reduce(f32[512]{0:T(512)S(1)} %psum.30), channel_id=1, replica_groups=mesh['paths'=16,'stocks'=8] {'paths'}, use_global_device_ids=true, to_apply=%region_12.13 | all-reduce | flops 512 | bytes 4096 | tf_op jit(solution)/shard_map/psum | solution.py:97
  175.2 30.4 %all-reduce.4.cloned.1.call-done = f32[512,512]{0,1:T(8,128)} async-done(((f32[512,512]{0,1:T(8,128)}), f32[512,512]{0,1:T(8,128)}) %all-reduce.4.cloned.1.call-update) | async-done | bytes 1048592 | tf_op jit(solution)/shard_map/psum | solution.py:97
  205.7 2.2 maximum_bitcast_fusion.1
  207.8 2.1 fusion.105
  209.9 116.2 %all-reduce.6.cloned.1.call-done = f32[512,512]{0,1:T(8,128)} async-done(((f32[512,512]{0,1:T(8,128)}), f32[512,512]{0,1:T(8,128)}) %all-reduce.6.cloned.1.call-update) | async-done | bytes 1048592 | tf_op jit(solution)/shard_map/psum | solution.py:97
  326.1 2.4 select_add_fusion
  328.5 1.6 copy.44
  330.3 1.0 copy-done.7
  331.3 11.7 %cholesky.103 = f32[128,128]{1,0:T(8,128)S(1)} custom-call(f32[128,128]{1,0:T(8,128)S(1)} %cholesky.263), custom_call_target="Cholesky" | custom-call | tf_op jit(solution)/shard_map/jit(cholesky)/cholesky | solution.py:66
  343.1 9.8 %custom-call.34 = f32[1,128,128]{1,2,0:T(8,128)S(1)} custom-call(f32[1,128,128]{2,1,0:T(8,128)S(1)} %get-tuple-element.52), custom_call_target="InvertDiagBlocksLowerTriangular" | custom-call | tf_op jit(solution)/shard_map/jit(cholesky)/cholesky | solution.py:66
  352.9 1.2 fusion.57
  354.1 1.3 convolution_subtract_fusion
  355.4 11.7 %cholesky.215 = f32[128,128]{1,0:T(8,128)S(1)} custom-call(f32[128,128]{1,0:T(8,128)S(1)} %cholesky.267), custom_call_target="Cholesky" | custom-call | tf_op jit(solution)/shard_map/jit(cholesky)/cholesky | solution.py:66
  367.8 9.8 %custom-call.35 = f32[1,128,128]{1,2,0:T(8,128)S(1)} custom-call(f32[1,128,128]{2,1,0:T(8,128)S(1)} %get-tuple-element.50), custom_call_target="InvertDiagBlocksLowerTriangular" | custom-call | tf_op jit(solution)/shard_map/jit(cholesky)/cholesky | solution.py:66
  377.9 1.5 convolution_subtract_fusion.1
  379.5 11.7 %cholesky.236 = f32[128,128]{1,0:T(8,128)S(1)} custom-call(f32[128,128]{1,0:T(8,128)S(1)} %cholesky.272), custom_call_target="Cholesky" | custom-call | tf_op jit(solution)/shard_map/jit(cholesky)/cholesky | solution.py:66
  391.3 9.8 %custom-call.36 = f32[1,128,128]{1,2,0:T(8,128)S(1)} custom-call(f32[1,128,128]{2,1,0:T(8,128)S(1)} %get-tuple-element.48), custom_call_target="InvertDiagBlocksLowerTriangular" | custom-call | tf_op jit(solution)/shard_map/jit(cholesky)/cholesky | solution.py:66
  401.4 1.3 convolution_subtract_fusion.2
  402.8 11.9 %cholesky.253 = f32[128,128]{1,0:T(8,128)S(1)} custom-call(f32[128,128]{1,0:T(8,128)S(1)} %convolution_subtract_fusion.2), custom_call_target="Cholesky" | custom-call | tf_op jit(solution)/shard_map/jit(cholesky)/cholesky | solution.py:66
  414.8 0.6 compare_reduce_fusion.1
  415.5 0.7 compare_reduce_fusion
  416.1 0.7 compare_reduce_fusion.2
  419.5 10.7 %while.1 = (s32[]{:T(128)}, f32[512,512]{0,1:T(8,128)S(1)}, s32[4,2]{0,1:T(2,128)S(1)}, f32[4,128,128]{2,1,0:T(8,128)}, s32[]{:T(128)}) while((s32[]{:T(128)}, f32[512,512]{0,1:T(8,128)S(1)}, s32[4,2]{0,1:T(2,128)S(1)}, f32[4,128,128]{2,1,0:T(8,128)}, s32[]{:T(128)}) %tuple.48), condition=%wide.while_cond, body=%wide.while_body.sunk | while | flops 2 | bytes 393829 | solution.py:67
  420.1 1.3 dynamic-slice.23
  421.5 0.6 bitcast_dynamic-update-slice_fusion.2
  422.8 1.3 dynamic-slice.23
  424.2 0.6 bitcast_dynamic-update-slice_fusion.2
  425.4 1.3 dynamic-slice.23
  426.9 0.6 bitcast_dynamic-update-slice_fusion.2
  428.1 1.3 dynamic-slice.23
  430.1 40.2 %custom-call.37 = f32[4,128,128]{1,2,0:T(8,128)S(1)} custom-call(f32[4,128,128]{2,1,0:T(8,128)} %get-tuple-element.9), custom_call_target="InvertDiagBlocksLowerTriangular" | custom-call | tf_op jit(solution)/shard_map/jit(_cho_solve)/triangular_solve | solution.py:67
  473.3 3.4 fusion.16
  477.9 0.7 copy-done.4
  478.6 1.1 fusion.20
  480.2 1.8 fusion.2
  482.0 1.1 fusion.26
  483.2 1.1 fusion.25
  484.3 2.6 fusion.24
  486.9 12.7 %all_to_all.44 = f32[16,256,16]{1,2,0:T(8,128)S(1)} all-to-all(f32[16,256,16]{1,2,0:T(8,128)S(1)} %bitcast.239), channel_id=1, replica_groups=mesh['paths'=16,'stocks'=8] {'paths'}, dimensions={0} | all-to-all | bytes 524288 | tf_op jit(solution)/shard_map/all_to_all | solution.py:20
  499.8 13.9 %all_to_all.45 = f32[8,1,512]{2,1,0:T(1,128)S(1)} all-to-all(f32[8,1,512]{2,1,0:T(1,128)S(1)} %reshape.229), channel_id=1, replica_groups=mesh['paths'=16,'stocks'=8] {'stocks'}, dimensions={0} | all-to-all | bytes 32768 | tf_op jit(solution)/shard_map/all_to_all | solution.py:20
  513.7 3.6 all-to-all-start.3
  517.9 0.7 reduce.24
  519.2 26.7 %all-to-all-done.3 = f32[8,32,2048]{2,1,0:T(8,128)S(1)} async-done(((f32[8,32,2048]{2,1,0:T(8,128)}), f32[8,32,2048]{2,1,0:T(8,128)S(1)}, u32[]{:S(2)}, u32[]{:S(2)}) %all-to-all-start.3) | async-done | bytes 2097184 | tf_op jit(solution)/shard_map/all_to_all | solution.py:127
  546.0 1.5 copy.60
  (111 shorter events, 12.9 us)
Async XLA Ops:
  7.2 1.2 copy-start
  11.1 38.3 %all-to-all-start.2 = ((f32[8,32,2048]{2,1,0:T(8,128)}), f32[8,32,2048]{2,1,0:T(8,128)}, u32[]{:S(2)}, u32[]{:S(2)}) async-start(f32[8,32,2048]{2,1,0:T(8,128)} %bitcast.220), calls=%async_computation.2 | async-start | bytes 4194304 | tf_op jit(solution)/shard_map/all_to_all | solution.py:20
  18.0 5.1 copy-start.10
  49.3 41.0 %all-to-all-start = ((bf16[8,5,16,2048]{3,2,1,0:T(8,128)(2,1)}), bf16[8,5,16,2048]{3,2,1,0:T(8,128)(2,1)S(1)}, u32[]{:S(2)}, u32[]{:S(2)}) async-start(bf16[8,5,16,2048]{3,2,1,0:T(8,128)(2,1)} %copy.40), calls=%async_computation | async-start | bytes 5242880 | tf_op jit(solution)/shard_map/all_to_all | solution.py:41
  90.4 115.3 %all-to-all-start.1 = ((bf16[8,5,16,2048]{3,2,1,0:T(8,128)(2,1)}), bf16[8,5,16,2048]{3,2,1,0:T(8,128)(2,1)}, u32[]{:S(2)}, u32[]{:S(2)}) async-start(bf16[8,5,16,2048]{3,2,1,0:T(8,128)(2,1)} %copy.41), calls=%async_computation.1 | async-start | bytes 5242880 | tf_op jit(solution)/shard_map/all_to_all | solution.py:41
  94.8 2.5 copy-start.19
  94.8 2.5 copy-start.20
  94.8 110.8 %all-reduce.4.cloned.1.call-start = ((), (), s32[]{:S(2)}) async-start(), calls=%async_computation.6 | async-start | bytes 2097152 | tf_op jit(solution)/shard_map/psum | solution.py:97
  101.1 1.3 copy-start.9
  102.5 2.5 dynamic-slice-start
  105.0 221.1 %all-reduce.6.cloned.1.call-start = ((), (), s32[]{:S(2)}) async-start(), calls=%async_computation.7 | async-start | bytes 2097152 | tf_op jit(solution)/shard_map/psum | solution.py:97
  326.1 4.0 copy-start.6
  330.3 1.0 copy-start.7
  430.1 46.6 %copy-start.5 = (bf16[1,8,32,2048]{3,2,0,1:T(8,128)(2,1)S(1)}, bf16[1,8,32,2048]{3,2,0,1:T(8,128)(2,1)}, u32[]{:S(2)}) copy-start(bf16[1,8,32,2048]{3,2,0,1:T(8,128)(2,1)} %get-tuple-element.36) | copy-start | bytes 3145732
  430.1 46.6 %copy-start.8 = (bf16[256,256]{1,0:T(8,128)(2,1)S(1)}, bf16[256,256]{1,0:T(8,128)(2,1)}, u32[]{:S(2)}) copy-start(bf16[256,256]{1,0:T(8,128)(2,1)} %param.20) | copy-start | bytes 393220
  430.1 46.6 %copy-start.18 = (f32[256]{0:T(256)S(1)}, f32[256]{0:T(256)}, u32[]{:S(2)}) copy-start(f32[256]{0:T(256)} %param.21) | copy-start | bytes 3076
  470.4 6.3 %copy-start.14 = (f32[1,2048]{1,0:T(1,128)S(1)}, f32[1,2048]{1,0:T(1,128)}, u32[]{:S(2)}) copy-start(f32[1,2048]{1,0:T(1,128)} %get-tuple-element.43) | copy-start | bytes 24580
  470.4 6.3 %copy-start.15 = (f32[1,2048]{1,0:T(1,128)S(1)}, f32[1,2048]{1,0:T(1,128)}, u32[]{:S(2)}) copy-start(f32[1,2048]{1,0:T(1,128)} %get-tuple-element.44) | copy-start | bytes 24580
  470.4 6.3 %copy-start.16 = (f32[1,2048]{1,0:T(1,128)S(1)}, f32[1,2048]{1,0:T(1,128)}, u32[]{:S(2)}) copy-start(f32[1,2048]{1,0:T(1,128)} %get-tuple-element.45) | copy-start | bytes 24580
  470.4 6.3 %copy-start.17 = (f32[1,2048]{1,0:T(1,128)S(1)}, f32[1,2048]{1,0:T(1,128)}, u32[]{:S(2)}) copy-start(f32[1,2048]{1,0:T(1,128)} %get-tuple-element.46) | copy-start | bytes 24580
  477.3 1.2 copy-start.4
  477.3 1.2 copy-start.13
  480.1 1.9 copy-start.3
  480.1 1.8 copy-start.12
  482.0 1.2 copy-start.2
  482.0 1.2 copy-start.11
  513.7 32.2 %all-to-all-start.3 = ((f32[8,32,2048]{2,1,0:T(8,128)}), f32[8,32,2048]{2,1,0:T(8,128)S(1)}, u32[]{:S(2)}, u32[]{:S(2)}) async-start(f32[8,32,2048]{2,1,0:T(8,128)} %bitcast.60), calls=%async_computation.3 | async-start | bytes 4194304 | tf_op jit(solution)/shard_map/all_to_all | solution.py:127
  546.0 1.6 copy-start.1
Sparse Core Ops, SparseCore 0:
  105.1 100.4 all-reduce.3
  208.1 117.9 all-reduce.5
